TPU v7x, 32 devices: a whole 2x2x4 slice. The times are simulated.
32 devices in a mesh: ctx: 4 (over z), exp: 8 (over y, x, core).
Axes of the slice: x: 2, y: 2, z: 4, core: 2. Of those that a mesh axis runs over, the one named last changes fastest.
Arguments:
- out_grad: bfloat16 [4096, 2048], P(('ctx', 'exp')), may hold values from -6 to 6
- route_ids: int32 [4096, 4], P(('ctx', 'exp')), may hold values from 0 to 15, all different within a row; in each aligned block of 128 rows (0 to 127, 128 to 255, ...) at most 36 rows name the same one
- gate_probs: float32 [4096, 4], P(('ctx', 'exp')), may hold values from 0 to 1, as said below
- saved_hidden: bfloat16 [4, 8, 16, 36, 768], P('ctx', None, 'exp'), may hold values from -6 to 6
- down_weight: bfloat16 [16, 768, 2048], P('exp', None, 'ctx'), may hold values from -0.02734375 to 0.02734375
- router_weight: bfloat16 [2048, 16], replicated, may hold values from -1.5 to 1.5
- proj_weight: bfloat16 [4096, 2048], P('ctx'), may hold values from -0.125 to 0.125
Outputs:
- head_grads: bfloat16 [4, 1024, 4096], P(None, 'exp', 'ctx')
- router_grad: float32 [4096, 4], P(('ctx', 'exp'))
Inputs may be any that keep to these rules, and one draw needn't show every extreme that they name: `route_ids`: each token names 4 different experts; among the tokens of one device no expert is named more than 36 times, and in some device some expert is named exactly 36 times. `gate_probs`: positive; a token's 4 gates sum to one.
All inputs are finite; a program needn't handle non-finite values.
Results may differ from a plain program's by a relative error of at most 0.009.
Values may be sent and summed in bfloat16 or wider, within the bound.
A program may use at most 64 MiB of HBM per device.

v0:
```python
import jax
import jax.numpy as jnp
from jax import lax
from jax.sharding import PartitionSpec as P


def route_ranks(route_ids, experts):
    flat_ids = route_ids.reshape(-1)
    onehot = (flat_ids[:, None] == jnp.arange(experts, dtype=jnp.int32)[None, :]).astype(jnp.int32)
    earlier = jnp.cumsum(onehot, axis=0) - onehot
    slot_rank = jnp.sum(earlier * onehot, axis=1)
    return (flat_ids, slot_rank)


def shards(out_grad, route_ids, gate_probs, saved_hidden, down_weight, router_weight, proj_weight):
    tok_rows, top_count = route_ids.shape
    experts = router_weight.shape[1]
    groups = lax.axis_size("exp")
    local_experts = down_weight.shape[0]
    capacity = saved_hidden.shape[3]
    arrived_rows = lax.all_gather(out_grad, "ctx", axis=0, tiled=True)
    flat_ids, slot_rank = route_ranks(route_ids, experts)
    positions = flat_ids * capacity + slot_rank
    hidden_local = saved_hidden[0]
    spread = jnp.repeat(out_grad, top_count, axis=0)
    send_rows = (
        jnp.zeros((experts * capacity, out_grad.shape[1]), out_grad.dtype).at[positions].set(spread)
    )
    send_rows = send_rows.reshape(groups, local_experts, capacity, out_grad.shape[1])
    arrived = lax.all_to_all(send_rows, "exp", split_axis=0, concat_axis=0, tiled=True)
    outputs = jnp.einsum(
        "secf,efn->secn",
        hidden_local,
        lax.all_gather(down_weight, "ctx", axis=2, tiled=True),
        preferred_element_type=jnp.float32,
    ).astype(jnp.bfloat16)
    partial_grad = jnp.sum(arrived.astype(jnp.float32) * outputs.astype(jnp.float32), axis=3)
    returned = lax.all_to_all(partial_grad, "exp", split_axis=0, concat_axis=0, tiled=True)
    gate_grad = returned.reshape(-1)[positions].reshape(tok_rows, top_count)
    weighted = jnp.sum(gate_probs * gate_grad, axis=1, keepdims=True)
    router_grad = gate_probs * (gate_grad - weighted)
    matches = route_ids[:, :, None] == jnp.arange(experts, dtype=jnp.int32)[None, None, :]
    dense_grad = jnp.sum(jnp.where(matches, router_grad[:, :, None], 0.0), axis=1)
    router_wide = router_weight.astype(jnp.float32)
    dense_all = lax.all_gather(dense_grad.astype(jnp.bfloat16), "ctx", axis=0, tiled=True).astype(
        dense_grad.dtype
    )
    combined = (
        arrived_rows.astype(jnp.float32)
        + lax.dot_general(
            dense_all, router_wide, (((1,), (1,)), ((), ())), precision=lax.Precision.HIGHEST
        )
    ).astype(jnp.bfloat16)
    head_flat = lax.dot_general(
        combined, proj_weight, (((1,), (1,)), ((), ())), preferred_element_type=jnp.float32
    ).astype(jnp.bfloat16)
    head_grads = head_flat.reshape(lax.axis_size("ctx"), tok_rows, proj_weight.shape[0])
    return (head_grads, router_grad)


def solution(mesh):
    return jax.shard_map(
        shards,
        mesh=mesh,
        in_specs=(
            P(("ctx", "exp"), None),
            P(("ctx", "exp"), None),
            P(("ctx", "exp"), None),
            P("ctx", None, "exp", None, None),
            P("exp", None, "ctx"),
            P(),
            P("ctx", None),
        ),
        out_specs=(P(None, "exp", "ctx"), P(("ctx", "exp"), None)),
        check_vma=False,
    )
```

profile of v0, /device:TPU:0, one launch (start us, length us, event | category | flops | bytes accessed | tf_op | source)
XLA Modules:
  0.0 186.4 jit_solution(17179931395707088919)
XLA Ops:
  7.2 0.7 all-gather.5.cloned.1.call-update
  7.9 0.8 copy.58
  8.9 1.2 reduce-window.6
  10.1 0.2 slice_reduce_fusion
  10.4 0.7 broadcast_multiply_fusion
  11.3 1.0 broadcast_in_dim.26
  12.3 2.1 %reshape.86 = bf16[512,2048]{1,0:T(8,128)(2,1)} reshape(bf16[128,4,2048]{2,1,0:T(4,128)(2,1)S(1)} %broadcast_in_dim.26) | data formatting | bytes 4194304 | tf_op jit(solution)/shard_map/reshape | solution.py:25
  14.6 6.3 %scatter_custom_fusion = bf16[576,2048]{1,0:T(8,128)(2,1)} fusion(s32[512]{0:T(512)S(1)} %bitcast.41, bf16[512,2048]{1,0:T(8,128)(2,1)} %reshape.86, bf16[]{:T(256)} %constant.5.clone.1), kind=kCustom, calls=%fused_computation.9 | custom fusion | bytes 2359808 | tf_op jit(solution)/shard_map/scatter | solution.py:27
  20.9 2.7 %reshape.70 = bf16[8,2,36,2048]{3,2,1,0:T(8,128)(2,1)S(1)} reshape(bf16[576,2048]{1,0:T(8,128)(2,1)} %scatter_custom_fusion) | data formatting | bytes 4718592 | tf_op jit(solution)/shard_map/reshape | solution.py:29
  23.6 3.9 %copy.61 = bf16[8,2,36,2048]{3,1,2,0:T(2,128)(2,1)} copy(bf16[8,2,36,2048]{3,2,1,0:T(8,128)(2,1)S(1)} %reshape.70) | data formatting | bytes 4718592 | tf_op jit(solution)/shard_map/reshape | solution.py:29
  27.5 5.2 %all-to-all-start = ((bf16[8,2,36,2048]{3,1,2,0:T(2,128)(2,1)}), bf16[8,2,36,2048]{3,1,2,0:T(2,128)(2,1)S(1)}, u32[]{:S(2)}, u32[]{:S(2)}) async-start(bf16[8,2,36,2048]{3,1,2,0:T(2,128)(2,1)} %copy.61), calls=%async_computation | async-start | bytes 4718592 | tf_op jit(solution)/shard_map/all_to_all | solution.py:30
  32.7 0.7 all-gather.3.cloned.1.call-update
  33.4 28.7 %all-to-all-done = bf16[8,2,36,2048]{3,1,2,0:T(2,128)(2,1)S(1)} async-done(((bf16[8,2,36,2048]{3,1,2,0:T(2,128)(2,1)}), bf16[8,2,36,2048]{3,1,2,0:T(2,128)(2,1)S(1)}, u32[]{:S(2)}, u32[]{:S(2)}) %all-to-all-start) | async-done | bytes 2359328 | tf_op jit(solution)/shard_map/all_to_all | solution.py:30
  62.1 65.6 %all-gather.5.cloned.1.call-done = bf16[2,768,2048]{2,1,0:T(8,128)(2,1)} async-done(((bf16[2,768,512]{2,1,0:T(8,128)(2,1)}), bf16[2,768,2048]{2,1,0:T(8,128)(2,1)}) %all-gather.5.cloned.1.call-update) | async-done | bytes 6291472 | tf_op jit(solution)/shard_map/all_gather | solution.py:34
  127.7 6.1 %fusion.2 = f32[8,2,36]{2,0,1:T(8,128)S(1)} fusion(bf16[8,2,36,2048]{3,1,2,0:T(2,128)(2,1)S(1)} %all-to-all-done, bf16[2,768,2048]{2,1,0:T(8,128)(2,1)} %all-gather.5.cloned.1.call-done, bf16[8,2,36,768]{3,1,2,0:T(2,128)(2,1)S(1)} %bitcast.40), kind=kOutput, calls=%fused_computation.5 | convolution fusion | flops 1817837056 | bytes 9537792 | tf_op jit(solution)/shard_map/secf,efn->secn/dot_general | solution.py:31
  133.8 0.6 copy.64
  134.4 3.8 %all-to-all-start.1 = ((f32[8,2,36]{2,1,0:T(2,128)}), f32[8,2,36]{2,1,0:T(2,128)S(1)}, u32[]{:S(2)}, u32[]{:S(2)}) async-start(f32[8,2,36]{2,1,0:T(2,128)} %copy.64), calls=%async_computation.1 | async-start | bytes 16384 | tf_op jit(solution)/shard_map/all_to_all | solution.py:38
  138.4 4.6 %all-to-all-done.1 = f32[8,2,36]{2,1,0:T(2,128)S(1)} async-done(((f32[8,2,36]{2,1,0:T(2,128)}), f32[8,2,36]{2,1,0:T(2,128)S(1)}, u32[]{:S(2)}, u32[]{:S(2)}) %all-to-all-start.1) | async-done | bytes 2336 | tf_op jit(solution)/shard_map/all_to_all | solution.py:38
  143.1 2.3 %gather_fusion = f32[512]{0:T(512)S(1)} fusion(f32[576]{0:T(1024)S(1)} %reshape.71, s32[1024]{0:T(1024)S(1)} %pad_clamp_fusion), kind=kCustom, calls=%fused_computation | custom fusion | bytes 6144 | tf_op jit(solution)/shard_map/gather | solution.py:39
  145.8 12.6 %all_gather.11 = bf16[512,16]{0,1:T(8,128)(2,1)S(1)} all-gather(bf16[128,16]{0,1:T(8,128)(2,1)S(1)} %select_reduce_fusion), channel_id=1, replica_groups=mesh['ctx'=4,'exp'=8] {'ctx'}, dimensions={0}, use_global_device_ids=true | all-gather | bytes 20480 | tf_op jit(solution)/shard_map/all_gather | solution.py:45
  158.4 15.0 %all-gather.3.cloned.1.call-done = bf16[512,2048]{1,0:T(8,128)(2,1)} async-done(((bf16[128,2048]{1,0:T(8,128)(2,1)}), bf16[512,2048]{1,0:T(8,128)(2,1)}) %all-gather.3.cloned.1.call-update) | async-done | bytes 2097168 | tf_op jit(solution)/shard_map/all_gather | solution.py:21
  173.4 2.5 %add_convert_fusion = bf16[512,2048]{1,0:T(8,128)(2,1)S(1)} fusion(bf16[512,2048]{1,0:T(8,128)(2,1)} %all-gather.3.cloned.1.call-done, bf16[512,16]{0,1:T(8,128)(2,1)S(1)} %all_gather.11, bf16[2048,16]{0,1:T(8,128)(2,1)S(1)} %copy-done.2), kind=kOutput, calls=%fused_computation.6 | convolution fusion | flops 36700160 | bytes 4276224 | tf_op jit(solution)/shard_map/dot_general | solution.py:50
  175.8 0.3 copy-done.6
  176.2 3.3 %convolution_convert_fusion = bf16[512,1024]{1,0:T(8,128)(2,1)} fusion(bf16[512,2048]{1,0:T(8,128)(2,1)S(1)} %add_convert_fusion, bf16[1024,2048]{1,0:T(8,128)(2,1)S(1)} %copy-done.6), kind=kOutput, calls=%fused_computation.8 | convolution fusion | flops 2148007936 | bytes 7340032 | tf_op jit(solution)/shard_map/dot_general | solution.py:54
  (32 shorter events, 1.3 us)
Async XLA Ops:
  7.2 120.5 %copy-start = (bf16[1,8,2,36,768]{4,2,3,1,0:T(2,128)(2,1)S(1)}, bf16[1,8,2,36,768]{4,2,3,1,0:T(2,128)(2,1)}, u32[]{:S(2)}) copy-start(bf16[1,8,2,36,768]{4,2,3,1,0:T(2,128)(2,1)} %param.10) | copy-start | bytes 2654212
  7.2 4.1 %copy-start.1 = (bf16[128,2048]{1,0:T(8,128)(2,1)S(1)}, bf16[128,2048]{1,0:T(8,128)(2,1)}, u32[]{:S(2)}) copy-start(bf16[128,2048]{1,0:T(8,128)(2,1)} %param.7) | copy-start | bytes 1572868
  7.2 120.5 %all-gather.5.cloned.1.call-start = ((), (), s32[]{:S(2)}) async-start(), calls=%async_computation.3 | async-start | bytes 7864320 | tf_op jit(solution)/shard_map/all_gather | solution.py:34
  27.5 34.6 %all-to-all-start = ((bf16[8,2,36,2048]{3,1,2,0:T(2,128)(2,1)}), bf16[8,2,36,2048]{3,1,2,0:T(2,128)(2,1)S(1)}, u32[]{:S(2)}, u32[]{:S(2)}) async-start(bf16[8,2,36,2048]{3,1,2,0:T(2,128)(2,1)} %copy.61), calls=%async_computation | async-start | bytes 4718592 | tf_op jit(solution)/shard_map/all_to_all | solution.py:30
  32.7 140.7 %all-gather.3.cloned.1.call-start = ((), (), s32[]{:S(2)}) async-start(), calls=%async_computation.2 | async-start | bytes 2621440 | tf_op jit(solution)/shard_map/all_gather | solution.py:21
  127.7 10.6 %copy-start.5 = (f32[128,4]{0,1:T(4,128)S(1)}, f32[128,4]{0,1:T(4,128)}, u32[]{:S(2)}) copy-start(f32[128,4]{0,1:T(4,128)} %param.9) | copy-start | bytes 6148
  133.8 11.9 %copy-start.3 = (s32[128,4]{0,1:T(4,128)S(1)}, s32[128,4]{0,1:T(4,128)}, u32[]{:S(2)}) copy-start(s32[128,4]{0,1:T(4,128)} %param.8) | copy-start | bytes 6148
  133.8 39.6 %copy-start.2 = (bf16[2048,16]{0,1:T(8,128)(2,1)S(1)}, bf16[2048,16]{0,1:T(8,128)(2,1)}, u32[]{:S(2)}) copy-start(bf16[2048,16]{0,1:T(8,128)(2,1)} %param.12) | copy-start | bytes 196612
  134.4 8.5 %all-to-all-start.1 = ((f32[8,2,36]{2,1,0:T(2,128)}), f32[8,2,36]{2,1,0:T(2,128)S(1)}, u32[]{:S(2)}, u32[]{:S(2)}) async-start(f32[8,2,36]{2,1,0:T(2,128)} %copy.64), calls=%async_computation.1 | async-start | bytes 16384 | tf_op jit(solution)/shard_map/all_to_all | solution.py:38
  145.7 33.8 %copy-start.4 = (f32[128,4]{0,1:T(4,128)}, f32[128,4]{0,1:T(4,128)S(1)}, u32[]{:S(2)}) copy-start(f32[128,4]{0,1:T(4,128)S(1)} %copy.67) | copy-start | bytes 6148
  173.4 2.8 %copy-start.6 = (bf16[1024,2048]{1,0:T(8,128)(2,1)S(1)}, bf16[1024,2048]{1,0:T(8,128)(2,1)}, u32[]{:S(2)}) copy-start(bf16[1024,2048]{1,0:T(8,128)(2,1)} %param.13) | copy-start | bytes 12582916
Sparse Core Ops, SparseCore 0:
  9.6 118.0 all-gather.4
  129.2 44.0 all-gather.2
where the time goes:
time: 187 us; the launch traced here: 186 us
  waiting for transfers between devices  115 us (61%)
  local copies, waits for them, and re-layouts  21.1 us (11%)
  between operations  14.2 us (8%)
  blocking collectives  12.6 us (7%)
  matrix products  11.9 us (6%)
  starting transfers between devices  9.12 us (5%)
  other arithmetic  2.22 us (1%)
    all_gather x1, waiting for transfers between devices, shards(): lax.all_gather(down_weight, 'ctx', axis=2, tiled=True)  65.6 us
    all_to_all x1, waiting for transfers between devices, shards(): lax.all_to_all(send_rows, 'exp', split_axis=0, concat_axis=0, tiled=True)  28.7 us
    all_gather x1, waiting for transfers between devices, shards(): arrived_rows = lax.all_gather(out_grad, 'ctx', axis=0, tiled=True)  15 us
    all_gather x1, blocking collectives, shards(): lax.all_gather(dense_grad.astype(jnp.bfloat16), 'ctx', axis=0, tiled=True)  12.6 us
    reshape x2, local copies, waits for them, and re-layouts, shards(): send_rows.reshape(groups, local_experts, capacity, out_grad.shape[1])  6.6 us
    scatter x1, local copies, waits for them, and re-layouts, shards(): jnp.zeros((experts * capacity, out_grad.shape[1]), out_grad.dtype)  6.29 us
    dot_general x1, matrix products, shards(): jnp.einsum('secf,efn->secn', hidden_local, lax.all_gather(down_weight, 'c...  6.13 us
    all_to_all x1, starting transfers between devices, shards(): lax.all_to_all(send_rows, 'exp', split_axis=0, concat_axis=0, tiled=True)  5.21 us
  transfers between devices with their start and end apart: 4, of which 4 were waited for; matrix products, arithmetic and copies ran while one was open for 16% of the time, Pallas kernels for 0%

commit v1 on v0

--- a/solution.py
+++ b/solution.py
@@ -42,9 +42,12 @@
     matches = route_ids[:, :, None] == jnp.arange(experts, dtype=jnp.int32)[None, None, :]
     dense_grad = jnp.sum(jnp.where(matches, router_grad[:, :, None], 0.0), axis=1)
     router_wide = router_weight.astype(jnp.float32)
-    dense_all = lax.all_gather(dense_grad.astype(jnp.bfloat16), "ctx", axis=0, tiled=True).astype(
-        dense_grad.dtype
-    )
+    dense_all = jnp.concatenate(
+        lax.all_to_all(
+            jnp.stack([dense_grad.astype(jnp.bfloat16)] * lax.axis_size("ctx")), "ctx", 0, 0
+        ),
+        axis=0,
+    ).astype(dense_grad.dtype)
     combined = (
         arrived_rows.astype(jnp.float32)
         + lax.dot_general(

time: 187 us -> 187 us (level)
  blocking collectives: 12.6 us -> 0 us
  waiting for transfers between devices: 115 us -> 124 us
  starting transfers between devices: 9.12 us -> 12.4 us
    all_gather x1 -> x0, blocking collectives: 12.6 us -> none  [shards(): lax.all_gather(dense_grad.astype(jnp.bfloat16), 'ctx', axis=0, tiled=True)]
    all_gather x1, waiting for transfers between devices: 15 us -> 23.6 us  [shards(): arrived_rows = lax.all_gather(out_grad, 'ctx', axis=0, tiled=True)]
    all_to_all x0 -> x1, starting transfers between devices: none -> 3.25 us  [shards(): lax.all_to_all(jnp.stack([dense_grad.astype(jnp.bfloat16)] * lax.axis_siz...]
  transfers between devices with their start and end apart: 4 -> 5, of which waited for: 4 -> 4; matrix products, arithmetic and copies ran while one was open for 16% -> 16% of each run, Pallas kernels for 0% -> 0%
where the time goes in v1:
time: 187 us; the launch traced here: 186 us
  waiting for transfers between devices  124 us (66%)
  local copies, waits for them, and re-layouts  21.7 us (12%)
  between operations  14.2 us (8%)
  starting transfers between devices  12.4 us (7%)
  matrix products  12.1 us (6%)
  other arithmetic  2.22 us (1%)
    all_gather x1, waiting for transfers between devices, shards(): lax.all_gather(down_weight, 'ctx', axis=2, tiled=True)  65.6 us
    all_to_all x1, waiting for transfers between devices, shards(): lax.all_to_all(send_rows, 'exp', split_axis=0, concat_axis=0, tiled=True)  28.7 us
    all_gather x1, waiting for transfers between devices, shards(): arrived_rows = lax.all_gather(out_grad, 'ctx', axis=0, tiled=True)  23.6 us
    reshape x2, local copies, waits for them, and re-layouts, shards(): send_rows.reshape(groups, local_experts, capacity, out_grad.shape[1])  6.6 us
    dot_general x1, matrix products, shards(): jnp.einsum('secf,efn->secn', hidden_local, lax.all_gather(down_weight, 'c...  6.34 us
    scatter x1, local copies, waits for them, and re-layouts, shards(): jnp.zeros((experts * capacity, out_grad.shape[1]), out_grad.dtype)  6.29 us
    all_to_all x1, starting transfers between devices, shards(): lax.all_to_all(send_rows, 'exp', split_axis=0, concat_axis=0, tiled=True)  5.2 us
    all_to_all x1, waiting for transfers between devices, shards(): lax.all_to_all(partial_grad, 'exp', split_axis=0, concat_axis=0, tiled=True)  4.58 us
  transfers between devices with their start and end apart: 5, of which 4 were waited for; matrix products, arithmetic and copies ran while one was open for 16% of the time, Pallas kernels for 0%

profile of v1, /device:TPU:0, one launch (start us, length us, event | category | flops | bytes accessed | tf_op | source)
XLA Modules:
  0.0 186.4 jit_solution(17586530756035697667)
XLA Ops:
  7.2 0.7 all-gather.5.cloned.1.call-update
  7.9 0.8 copy.60
  8.9 1.2 reduce-window.6
  10.4 0.7 broadcast_multiply_fusion
  11.3 1.0 broadcast_in_dim.26
  12.3 2.1 %reshape.92 = bf16[512,2048]{1,0:T(8,128)(2,1)} reshape(bf16[128,4,2048]{2,1,0:T(4,128)(2,1)S(1)} %broadcast_in_dim.26) | data formatting | bytes 4194304 | tf_op jit(solution)/shard_map/reshape | solution.py:25
  14.6 6.3 %scatter_custom_fusion = bf16[576,2048]{1,0:T(8,128)(2,1)} fusion(s32[512]{0:T(512)S(1)} %bitcast.47, bf16[512,2048]{1,0:T(8,128)(2,1)} %reshape.92, bf16[]{:T(256)} %constant.5.clone.1), kind=kCustom, calls=%fused_computation.9 | custom fusion | bytes 2359808 | tf_op jit(solution)/shard_map/scatter | solution.py:27
  20.8 2.7 %reshape.75 = bf16[8,2,36,2048]{3,2,1,0:T(8,128)(2,1)S(1)} reshape(bf16[576,2048]{1,0:T(8,128)(2,1)} %scatter_custom_fusion) | data formatting | bytes 4718592 | tf_op jit(solution)/shard_map/reshape | solution.py:29
  23.6 3.8 %copy.63 = bf16[8,2,36,2048]{3,1,2,0:T(2,128)(2,1)} copy(bf16[8,2,36,2048]{3,2,1,0:T(8,128)(2,1)S(1)} %reshape.75) | data formatting | bytes 4718592 | tf_op jit(solution)/shard_map/reshape | solution.py:29
  27.5 5.2 %all-to-all-start = ((bf16[8,2,36,2048]{3,1,2,0:T(2,128)(2,1)}), bf16[8,2,36,2048]{3,1,2,0:T(2,128)(2,1)S(1)}, u32[]{:S(2)}, u32[]{:S(2)}) async-start(bf16[8,2,36,2048]{3,1,2,0:T(2,128)(2,1)} %copy.63), calls=%async_computation | async-start | bytes 4718592 | tf_op jit(solution)/shard_map/all_to_all | solution.py:30
  32.7 0.7 all-gather.3.cloned.1.call-update
  33.4 28.7 %all-to-all-done = bf16[8,2,36,2048]{3,1,2,0:T(2,128)(2,1)S(1)} async-done(((bf16[8,2,36,2048]{3,1,2,0:T(2,128)(2,1)}), bf16[8,2,36,2048]{3,1,2,0:T(2,128)(2,1)S(1)}, u32[]{:S(2)}, u32[]{:S(2)}) %all-to-all-start) | async-done | bytes 2359328 | tf_op jit(solution)/shard_map/all_to_all | solution.py:30
  62.1 65.6 %all-gather.5.cloned.1.call-done = bf16[2,768,2048]{2,1,0:T(8,128)(2,1)} async-done(((bf16[2,768,512]{2,1,0:T(8,128)(2,1)}), bf16[2,768,2048]{2,1,0:T(8,128)(2,1)}) %all-gather.5.cloned.1.call-update) | async-done | bytes 6291472 | tf_op jit(solution)/shard_map/all_gather | solution.py:34
  127.7 6.3 %fusion.2 = f32[8,2,36]{2,0,1:T(8,128)S(1)} fusion(bf16[8,2,36,2048]{3,1,2,0:T(2,128)(2,1)S(1)} %all-to-all-done, bf16[2,768,2048]{2,1,0:T(8,128)(2,1)} %all-gather.5.cloned.1.call-done, bf16[8,2,36,768]{3,1,2,0:T(2,128)(2,1)S(1)} %bitcast.46), kind=kOutput, calls=%fused_computation.5 | convolution fusion | flops 1817837056 | bytes 9537792 | tf_op jit(solution)/shard_map/secf,efn->secn/dot_general | solution.py:31
  134.0 0.6 copy.66
  134.6 3.8 %all-to-all-start.1 = ((f32[8,2,36]{2,1,0:T(2,128)}), f32[8,2,36]{2,1,0:T(2,128)S(1)}, u32[]{:S(2)}, u32[]{:S(2)}) async-start(f32[8,2,36]{2,1,0:T(2,128)} %copy.66), calls=%async_computation.1 | async-start | bytes 16384 | tf_op jit(solution)/shard_map/all_to_all | solution.py:38
  138.6 4.6 %all-to-all-done.1 = f32[8,2,36]{2,1,0:T(2,128)S(1)} async-done(((f32[8,2,36]{2,1,0:T(2,128)}), f32[8,2,36]{2,1,0:T(2,128)S(1)}, u32[]{:S(2)}, u32[]{:S(2)}) %all-to-all-start.1) | async-done | bytes 2336 | tf_op jit(solution)/shard_map/all_to_all | solution.py:38
  143.3 2.3 %gather_fusion = f32[512]{0:T(512)S(1)} fusion(f32[576]{0:T(1024)S(1)} %reshape.76, s32[1024]{0:T(1024)S(1)} %pad_clamp_fusion), kind=kCustom, calls=%fused_computation | custom fusion | bytes 6144 | tf_op jit(solution)/shard_map/gather | solution.py:39
  146.0 0.6 stack.2
  146.6 3.3 %all-to-all-start.2 = ((bf16[4,128,16]{1,2,0:T(8,128)(2,1)}), bf16[4,128,16]{1,2,0:T(8,128)(2,1)S(1)}, u32[]{:S(2)}, u32[]{:S(2)}) async-start(bf16[4,128,16]{1,2,0:T(8,128)(2,1)} %stack.2), calls=%async_computation.2 | async-start | bytes 32768 | tf_op jit(solution)/shard_map/all_to_all | solution.py:46
  149.8 23.6 %all-gather.3.cloned.1.call-done = bf16[512,2048]{1,0:T(8,128)(2,1)} async-done(((bf16[128,2048]{1,0:T(8,128)(2,1)}), bf16[512,2048]{1,0:T(8,128)(2,1)}) %all-gather.3.cloned.1.call-update) | async-done | bytes 2097168 | tf_op jit(solution)/shard_map/all_gather | solution.py:21
  173.5 2.5 %add_convert_fusion = bf16[512,2048]{1,0:T(8,128)(2,1)S(1)} fusion(bf16[512,2048]{1,0:T(8,128)(2,1)} %all-gather.3.cloned.1.call-done, bf16[2048,16]{0,1:T(8,128)(2,1)S(1)} %copy-done.2, bf16[4,128,16]{1,2,0:T(8,128)(2,1)S(1)} %all-to-all-done.2), kind=kOutput, calls=%fused_computation.6 | convolution fusion | flops 36700160 | bytes 4276224 | tf_op jit(solution)/shard_map/dot_general | solution.py:53
  175.9 0.3 copy-done.6
  176.3 3.3 %convolution_convert_fusion = bf16[512,1024]{1,0:T(8,128)(2,1)} fusion(bf16[512,2048]{1,0:T(8,128)(2,1)S(1)} %add_convert_fusion, bf16[1024,2048]{1,0:T(8,128)(2,1)S(1)} %copy-done.6), kind=kOutput, calls=%fused_computation.8 | convolution fusion | flops 2148007936 | bytes 7340032 | tf_op jit(solution)/shard_map/dot_general | solution.py:57
  (34 shorter events, 1.5 us)
Async XLA Ops:
  7.2 120.5 %copy-start = (bf16[1,8,2,36,768]{4,2,3,1,0:T(2,128)(2,1)S(1)}, bf16[1,8,2,36,768]{4,2,3,1,0:T(2,128)(2,1)}, u32[]{:S(2)}) copy-start(bf16[1,8,2,36,768]{4,2,3,1,0:T(2,128)(2,1)} %param.10) | copy-start | bytes 2654212
  7.2 4.1 %copy-start.1 = (bf16[128,2048]{1,0:T(8,128)(2,1)S(1)}, bf16[128,2048]{1,0:T(8,128)(2,1)}, u32[]{:S(2)}) copy-start(bf16[128,2048]{1,0:T(8,128)(2,1)} %param.7) | copy-start | bytes 1572868
  7.2 120.5 %all-gather.5.cloned.1.call-start = ((), (), s32[]{:S(2)}) async-start(), calls=%async_computation.4 | async-start | bytes 7864320 | tf_op jit(solution)/shard_map/all_gather | solution.py:34
  27.5 34.6 %all-to-all-start = ((bf16[8,2,36,2048]{3,1,2,0:T(2,128)(2,1)}), bf16[8,2,36,2048]{3,1,2,0:T(2,128)(2,1)S(1)}, u32[]{:S(2)}, u32[]{:S(2)}) async-start(bf16[8,2,36,2048]{3,1,2,0:T(2,128)(2,1)} %copy.63), calls=%async_computation | async-start | bytes 4718592 | tf_op jit(solution)/shard_map/all_to_all | solution.py:30
  32.7 140.8 %all-gather.3.cloned.1.call-start = ((), (), s32[]{:S(2)}) async-start(), calls=%async_computation.3 | async-start | bytes 2621440 | tf_op jit(solution)/shard_map/all_gather | solution.py:21
  127.7 10.8 %copy-start.5 = (f32[128,4]{0,1:T(4,128)S(1)}, f32[128,4]{0,1:T(4,128)}, u32[]{:S(2)}) copy-start(f32[128,4]{0,1:T(4,128)} %param.9) | copy-start | bytes 6148
  134.0 11.9 %copy-start.3 = (s32[128,4]{0,1:T(4,128)S(1)}, s32[128,4]{0,1:T(4,128)}, u32[]{:S(2)}) copy-start(s32[128,4]{0,1:T(4,128)} %param.8) | copy-start | bytes 6148
  134.0 39.4 %copy-start.2 = (bf16[2048,16]{0,1:T(8,128)(2,1)S(1)}, bf16[2048,16]{0,1:T(8,128)(2,1)}, u32[]{:S(2)}) copy-start(bf16[2048,16]{0,1:T(8,128)(2,1)} %param.12) | copy-start | bytes 196612
  134.6 8.5 %all-to-all-start.1 = ((f32[8,2,36]{2,1,0:T(2,128)}), f32[8,2,36]{2,1,0:T(2,128)S(1)}, u32[]{:S(2)}, u32[]{:S(2)}) async-start(f32[8,2,36]{2,1,0:T(2,128)} %copy.66), calls=%async_computation.1 | async-start | bytes 16384 | tf_op jit(solution)/shard_map/all_to_all | solution.py:38
  145.9 33.7 %copy-start.4 = (f32[128,4]{0,1:T(4,128)}, f32[128,4]{0,1:T(4,128)S(1)}, u32[]{:S(2)}) copy-start(f32[128,4]{0,1:T(4,128)S(1)} %copy.69) | copy-start | bytes 6148
  146.6 26.9 %all-to-all-start.2 = ((bf16[4,128,16]{1,2,0:T(8,128)(2,1)}), bf16[4,128,16]{1,2,0:T(8,128)(2,1)S(1)}, u32[]{:S(2)}, u32[]{:S(2)}) async-start(bf16[4,128,16]{1,2,0:T(8,128)(2,1)} %stack.2), calls=%async_computation.2 | async-start | bytes 32768 | tf_op jit(solution)/shard_map/all_to_all | solution.py:46
  173.4 2.8 %copy-start.6 = (bf16[1024,2048]{1,0:T(8,128)(2,1)S(1)}, bf16[1024,2048]{1,0:T(8,128)(2,1)}, u32[]{:S(2)}) copy-start(bf16[1024,2048]{1,0:T(8,128)(2,1)} %param.13) | copy-start | bytes 12582916
Sparse Core Ops, SparseCore 0:
  9.6 118.0 all-gather.4
  129.2 44.1 all-gather.2
